TPU v7x, 32 devices: a whole 2x2x4 slice. The times are simulated.
32 devices in a mesh: tm: 2 (over y), aux: 16 (over z, x, core).
Axes of the slice: x: 2, y: 2, z: 4, core: 2. Of those that a mesh axis runs over, the one named last changes fastest.
Arguments:
- green: bfloat16 [4, 1024, 1024], P('tm'), may hold values from -4 to 4
- factors: bfloat16 [4096, 1024], P('aux'), may hold values from -0.1875 to 0.1875
- pattern: int32 [32, 8], P('aux'), may hold values 0 or 1
- coulomb: float32 [4096], P('aux'), may hold values from 0.5 to 2
Outputs:
- sigma: float32 [1024, 4, 1024], P('aux', 'tm')
All inputs are finite; a program needn't handle non-finite values. No bound on the sum of `pattern` on one device may be relied on, other than what follows from the above.
Results may differ from a plain program's by a relative error of at most 0.006.
Values may be sent and summed in bfloat16 or wider, within the bound.
A program may use at most 64 MiB of HBM per device.

v0:
```python
import jax
import jax.numpy as jnp
from jax import lax
from jax.sharding import PartitionSpec as P

BLOCK = 128


def swapped(value, axis, distance):
    return lax.ppermute(value, axis, [(i, i ^ 1 << distance) for i in range(lax.axis_size(axis))])


def mirrored_factor(values):
    top_bit = lax.axis_size("tm").bit_length() - 2
    return swapped(values, "tm", top_bit)


def local(green, factors, pattern, coulomb):
    mask = jnp.repeat(jnp.repeat(pattern, BLOCK, axis=0), BLOCK, axis=1)
    masked = factors * mask.astype(factors.dtype)
    left = jnp.einsum("po,tok->tpk", masked, green, preferred_element_type=jnp.float32).astype(
        jnp.bfloat16
    )
    own_right = jnp.einsum("po,tko->tpk", masked, green, preferred_element_type=jnp.float32).astype(
        jnp.bfloat16
    )
    right = mirrored_factor(own_right)
    rows = lax.all_gather(masked, "aux", axis=0, tiled=True)
    weights = lax.all_gather(coulomb.astype(jnp.bfloat16), "aux", axis=0, tiled=True).astype(
        jnp.float32
    )
    aux_green = jnp.einsum("tpo,qo->tpq", left, rows, preferred_element_type=jnp.float32)
    mirror = jnp.einsum("tpo,qo->tpq", right, rows, preferred_element_type=jnp.float32)
    chi = -aux_green * mirror
    kernel = (aux_green * coulomb[None, :, None] * chi * weights[None, None, :]).astype(
        jnp.bfloat16
    )
    summed = jnp.einsum("tpq,qo->tpo", kernel, rows, preferred_element_type=jnp.float32)
    carried = summed.astype(jnp.bfloat16)
    return lax.psum_scatter(
        -jnp.einsum("pi,tpj->itj", masked, carried, preferred_element_type=jnp.float32),
        "aux",
        scatter_dimension=0,
        tiled=True,
    )


def solution(mesh):
    in_specs = (P("tm", None, None), P("aux", None), P("aux", None), P("aux"))
    out_specs = P("aux", "tm", None)
    return jax.shard_map(local, mesh=mesh, in_specs=in_specs, out_specs=out_specs, check_vma=False)
```

profile of v0, /device:TPU:0, one launch (start us, length us, event | category | flops | bytes accessed | tf_op | source)
XLA Modules:
  0.0 232.6 jit_solution(11605255183256161217)
XLA Ops:
  6.5 0.0 copy-start.1
  6.5 0.0 all-gather.3.cloned.1.call-start
  6.5 0.7 convert_element_type.35
  7.2 0.3 broadcast_in_dim.9
  7.6 1.9 bitcast_multiply_fusion
  9.5 0.0 copy-start
  9.5 0.0 all-gather.3.cloned.1.call-update
  9.5 0.0 reduce-scatter.2.cloned.1.call-start
  9.6 3.7 %convolution_convert_fusion = bf16[256,2,1024]{2,0,1:T(8,128)(2,1)S(1)} fusion(bf16[2,1024,1024]{2,1,0:T(8,128)(2,1)} %param.4, bf16[256,1024]{1,0:T(8,128)(2,1)} %bitcast_multiply_fusion), kind=kOutput, calls=%fused_computation.9 | convolution fusion | flops 1074266112 | bytes 5767168 | tf_op jit(solution)/shard_map/po,tko->tpk/dot_general | solution.py:24
  13.2 1.1 copy.19
  14.3 3.1 %collective-permute-start = (bf16[2,256,1024]{2,0,1:T(2,128)(2,1)S(1)}, bf16[2,256,1024]{2,0,1:T(2,128)(2,1)S(1)}, u32[]{:S(2)}, u32[]{:S(2)}) collective-permute-start(bf16[2,256,1024]{2,0,1:T(2,128)(2,1)S(1)} %bitcast.47), channel_id=1, source_target_pairs={{0,16},{16,0},{1,17},{17,1},{2,18},{18,2},{3,19},{19,3},{4,20},{20... | collective-permute-start | bytes 3145736 | tf_op jit(solution)/shard_map/ppermute | solution.py:10
  17.4 0.0 copy-done.1
  17.4 22.4 %all-gather = bf16[16,1,256]{2,1,0:T(2,128)(2,1)S(1)} all-gather(bf16[1,1,256]{2,1,0:T(2,128)(2,1)S(1)} %reshape.6), channel_id=1, replica_groups=mesh['tm'=2,'aux'=16] {'aux'}, dimensions={0}, use_global_device_ids=true | all-gather | bytes 8704 | tf_op jit(solution)/shard_map/all_gather | solution.py:29
  39.9 46.9 %all-gather.3.cloned.1.call-done = bf16[4096,1024]{1,0:T(8,128)(2,1)} async-done(((bf16[256,1024]{1,0:T(8,128)(2,1)}), bf16[4096,1024]{1,0:T(8,128)(2,1)}) %all-gather.3.cloned.1.call-update) | async-done | bytes 8388624 | tf_op jit(solution)/shard_map/all_gather | solution.py:28
  86.8 0.0 copy-done
  86.8 12.4 %fusion.4 = f32[2,256,4096]{2,1,0:T(8,128)} fusion(bf16[4096,1024]{1,0:T(8,128)(2,1)} %all-gather.3.cloned.1.call-done, bf16[2,1024,1024]{2,1,0:T(8,128)(2,1)} %param.4, bf16[256,1024]{1,0:T(8,128)(2,1)S(1)} %copy-done), kind=kOutput, calls=%fused_computation.4 | convolution fusion | flops 5369233408 | bytes 21495808 | tf_op jit(solution)/shard_map/tpo,qo->tpq/dot_general | solution.py:32
  99.1 0.0 collective-permute-done
  99.1 10.6 %multiply_convert_fusion = bf16[2,256,4096]{2,1,0:T(8,128)(2,1)S(1)} fusion(f32[2,256,4096]{2,1,0:T(8,128)} %fusion.4, bf16[4096,1024]{1,0:T(8,128)(2,1)} %all-gather.3.cloned.1.call-done, f32[4096]{0:T(1024)S(1)} %bitcast.49, f32[256]{0:T(256)S(1)} %copy-done.1, bf16[2,256,1024]{2,0,1:T(2,128)(2,1)S(1)} %collective-permute-done), kind=kOutput, calls=%fused_computation.6 | convolution fusion | flops 4307550208 | bytes 22037504 | tf_op jit(solution)/shard_map/tpo,qo->tpq/dot_general | solution.py:33
  109.8 7.1 %fusion.8 = bf16[2,256,1024]{2,1,0:T(8,128)(2,1)S(1)} fusion(bf16[2,256,4096]{2,1,0:T(8,128)(2,1)S(1)} %multiply_convert_fusion, bf16[4096,1024]{1,0:T(8,128)(2,1)} %all-gather.3.cloned.1.call-done), kind=kOutput, calls=%fused_computation.8 | convolution fusion | flops 4295491584 | bytes 13631488 | tf_op jit(solution)/shard_map/tpq,qo->tpo/dot_general | solution.py:38
  116.9 4.5 %convolution_negate_fusion = f32[1024,2,1024]{2,0,1:T(8,128)} fusion(bf16[2,256,1024]{2,1,0:T(8,128)(2,1)S(1)} %fusion.8, bf16[256,1024]{1,0:T(8,128)(2,1)S(1)} %copy-done), kind=kOutput, calls=%fused_computation.7 | convolution fusion | flops 1075838976 | bytes 9961472 | tf_op jit(solution)/shard_map/pi,tpj->itj/dot_general | solution.py:41
  121.4 0.0 reduce-scatter.2.cloned.1.call-update
  121.4 102.1 %reduce-scatter.2.cloned.1.call-done = f32[64,2,1024]{2,0,1:T(8,128)} async-done(((f32[1024,2,1024]{2,0,1:T(8,128)}), f32[64,2,1024]{2,0,1:T(8,128)}) %reduce-scatter.2.cloned.1.call-update) | async-done | bytes 524304 | tf_op jit(solution)/shard_map/reduce_scatter | solution.py:40
  223.5 2.2 copy.8
  (4 shorter events, 0.0 us)
Async XLA Ops:
  6.5 10.9 %copy-start.1 = (f32[256]{0:T(256)S(1)}, f32[256]{0:T(256)}, u32[]{:S(2)}) copy-start(f32[256]{0:T(256)} %param.7) | copy-start | bytes 3076
  6.5 80.2 %all-gather.3.cloned.1.call-start = ((), (), s32[]{:S(2)}) async-start(), calls=%async_computation.1 | async-start | bytes 8912896 | tf_op jit(solution)/shard_map/all_gather | solution.py:28
  9.5 77.3 %copy-start = (bf16[256,1024]{1,0:T(8,128)(2,1)S(1)}, bf16[256,1024]{1,0:T(8,128)(2,1)}, u32[]{:S(2)}) copy-start(bf16[256,1024]{1,0:T(8,128)(2,1)} %bitcast_multiply_fusion) | copy-start | bytes 1572868
  9.5 214.0 %reduce-scatter.2.cloned.1.call-start = ((), (), s32[]{:S(2)}) async-start(), calls=%async_computation.2 | async-start | bytes 8912896 | tf_op jit(solution)/shard_map/reduce_scatter | solution.py:40
  14.3 84.8 %collective-permute-start = (bf16[2,256,1024]{2,0,1:T(2,128)(2,1)S(1)}, bf16[2,256,1024]{2,0,1:T(2,128)(2,1)S(1)}, u32[]{:S(2)}, u32[]{:S(2)}) collective-permute-start(bf16[2,256,1024]{2,0,1:T(2,128)(2,1)S(1)} %bitcast.47), channel_id=1, source_target_pairs={{0,16},{16,0},{1,17},{17,1},{2,18},{18,2},{3,19},{19,3},{4,20},{20... | collective-permute-start | bytes 3145736 | tf_op jit(solution)/shard_map/ppermute | solution.py:10
Sparse Core Ops, SparseCore 0:
  9.6 77.0 all-gather.2
  121.5 101.9 reduce-scatter.1
where the time goes:
time: 233 us
  waiting for transfers between devices  149 us (64%)
  matrix products  38.3 us (16%)
  blocking collectives  22.4 us (10%)
  between operations  13.4 us (6%)
  local copies, waits for them, and re-layouts  3.68 us (2%)
  starting transfers between devices  3.1 us (1%)
  other arithmetic  2.62 us (1%)
    reduce_scatter x1, waiting for transfers between devices, local(): lax.psum_scatter(-jnp.einsum('pi,tpj->itj', masked, carried, preferred_el...  102 us
    all_gather x1, waiting for transfers between devices, local(): rows = lax.all_gather(masked, 'aux', axis=0, tiled=True)  46.9 us
    all_gather x1, blocking collectives, local(): lax.all_gather(coulomb.astype(jnp.bfloat16), 'aux', axis=0, tiled=True)  22.4 us
    dot_general x1, matrix products, local(): jnp.einsum('tpo,qo->tpq', left, rows, preferred_element_type=jnp.float32)  12.4 us
    dot_general x1, matrix products, local(): jnp.einsum('tpo,qo->tpq', right, rows, preferred_element_type=jnp.float32)  10.6 us
    dot_general x1, matrix products, local(): jnp.einsum('tpq,qo->tpo', kernel, rows, preferred_element_type=jnp.float32)  7.07 us
  transfers between devices with their start and end apart: 3, of which 2 were waited for; matrix products, arithmetic and copies ran while one was open for 7% of the time, Pallas kernels for 0%

commit v1 on v0

v1 whole, which is shorter than its diff:
```python
import functools

import jax
import jax.numpy as jnp
from jax import lax
from jax.experimental import pallas as pl
from jax.experimental.pallas import tpu as pltpu
from jax.sharding import PartitionSpec as P

MESH = pl.DeviceIdType.MESH
F32, BF16 = jnp.float32, jnp.bfloat16


def turned(p):
    return p + lax.div(p, 2) * (1 - 2 * lax.rem(p, 2))


def dot(a, b, da, db):
    return lax.dot_general(a, b, (((da,), (db,)), ((), ())), preferred_element_type=F32)


def kernel(cfg, pattern, factors, coul, green_hbm, out, own, rows, weights, green, left_right,
           own_right, cp, kern, sig, csend, crecv, xsend, xrecv, zsend, zrecv, fin,
           gsem, ring_s, ring_r, x_s, x_r, cc_s, cc_r, cx_s, cx_r, tm_s, tm_r,
           rc_s, rc_r, rx_s, rx_r, rz_s, rz_r):
    Z, X, JH = cfg
    T, O = green.shape[0], green.shape[1]
    R = own.shape[0]
    JW = O // JH
    OUT = out.shape[1]
    tms = lax.axis_size("tm")
    a, tmi = lax.axis_index("aux"), lax.axis_index("tm")
    c = lax.rem(a, 2)
    x = lax.rem(lax.div(a, 2), X)
    z = lax.div(a, 2 * X)
    pos = turned(z)

    def dev(z_, x_, c_):
        return (z_ * X + x_) * 2 + c_

    def xo(e):
        return lax.rem(x + e, X)

    def zo(f):
        return lax.rem(z + f, Z)

    partner = lax.rem(tmi + tms // 2, tms)
    sibling = dev(z, x, 1 - c)
    sent = []

    def send(src, dst, s, r, **where):
        copy = pltpu.make_async_remote_copy(
            src_ref=src, dst_ref=dst, send_sem=s, recv_sem=r,
            device_id=where, device_id_type=MESH)
        copy.start()
        sent.append(copy)
        return copy

    loads = [pltpu.make_async_copy(green_hbm.at[t], green.at[t], gsem.at[t]) for t in range(T)]
    for copy in loads:
        copy.start()

    here = pl.multiple_of(a * R, R)
    brows = R // pattern.shape[0]
    bcols = O // pattern.shape[1]
    for i in range(pattern.shape[0]):
        for j in range(pattern.shape[1]):
            rs, cs = pl.ds(i * brows, brows), pl.ds(j * bcols, bcols)
            own[rs, cs] = (factors[rs, cs].astype(F32) * pattern[i, j].astype(F32)).astype(BF16)
    rows[pl.ds(here, R), :] = own[...]
    weights[a] = coul[...]
    cp[...] = jnp.transpose(jnp.broadcast_to(coul[...], (R, R)))

    barrier = pltpu.get_barrier_semaphore()
    friends = [{"aux": dev(zo(f), x, c)} for f in range(1, Z)]
    friends += [{"aux": dev(z, xo(e), c)} for e in range(1, X)]
    friends += [{"aux": sibling}, {"tm": partner}]
    for where in friends:
        pl.semaphore_signal(barrier, inc=1, device_id=where, device_id_type=MESH)
    pl.semaphore_wait(barrier, len(friends))

    nextd = dev(turned(lax.rem(pos + 1, Z)), x, c)

    def col_owner(k):
        return dev(turned(lax.rem(pos + Z - k, Z)), x, c)

    def xin_owner(k, e):
        return dev(turned(lax.rem(pos + Z - k, Z)), lax.rem(x + X - e, X), c)

    def pass_on(owner, s, r, to, first=False):
        at = pl.ds(pl.multiple_of(owner * R, R), R)
        src_rows = own if first else rows.at[at]
        src_w = coul if first else weights.at[owner]
        return [send(src_rows, rows.at[at], s.at[0], r.at[0], aux=to),
                send(src_w, weights.at[owner], s.at[1], r.at[1], aux=to)]

    ring, xs, ccs, cxs = {}, {}, {}, {}

    def wait_all(copies):
        for copy in copies:
            copy.wait_recv()

    def col_ready(k):
        if k > 0:
            wait_all(ring[k])
        owner = col_owner(k)
        if k < Z - 1:
            ring[k + 1] = pass_on(owner, ring_s.at[k], ring_r.at[k], nextd, k == 0)
        for e in range(1, X):
            xs[k, e] = pass_on(owner, x_s.at[k, e - 1], x_r.at[k, e - 1], dev(z, xo(e), c), k == 0)
        ccs[k] = pass_on(owner, cc_s.at[k], cc_r.at[k], sibling, k == 0)

    def xin_ready(k):
        for e in range(1, X):
            wait_all(xs[k, e])
            cxs[k, e] = pass_on(xin_owner(k, e), cx_s.at[k, e - 1], cx_r.at[k, e - 1], sibling)

    waited = set()

    def once(key, copies):
        if key not in waited:
            waited.add(key)
            wait_all(copies)

    def blocks(owner, ts):
        def one(i, carry):
            who = owner - c + lax.rem(c + lax.div(i, len(ts)), 2)
            t = ts[0] + lax.rem(i, len(ts))
            at = pl.ds(pl.multiple_of(who * R, R), R)
            both = dot(left_right[t], rows[at, :], 1, 1)
            ag, mirror = both[:R], both[R:]
            kern[t, :, at] = (ag * ag * mirror * (cp[...] * weights[who])).astype(BF16)
            return carry
        lax.fori_loop(0, 2 * len(ts), one, 0)

    def do_col(k, ts):
        once(("c", k), ccs[k])
        blocks(col_owner(k), ts)

    def do_xin(k, ts):
        for e in range(1, X):
            once(("x", k, e), cxs[k, e])
            blocks(xin_owner(k, e), ts)

    rights = {}

    def project_right(t):
        loads[t].wait()

        def one(j, carry):
            at = pl.ds(pl.multiple_of(j * 256, 256), 256)
            own_right[t, :, at] = dot(own[...], green[t, at, :], 1, 1).astype(BF16)
            return carry
        lax.fori_loop(0, O // 256, one, 0)
        rights[t] = send(own_right.at[t], left_right.at[t, pl.ds(R, R)], tm_s.at[t], tm_r.at[t],
                         tm=partner)

    def project_left(t):
        def one(j, carry):
            at = pl.ds(pl.multiple_of(j * 256, 256), 256)
            left_right[t, pl.ds(0, R), at] = dot(own[...], green[t, :, at], 1, 0).astype(BF16)
            return carry
        lax.fori_loop(0, O // 256, one, 0)

    col_ready(0)
    for t in range(T):
        project_right(t)
    for t in range(T):
        project_left(t)
    col_ready(1)
    xin_ready(0)
    rights[0].wait_recv()
    do_col(0, (0,))
    do_col(1, (0,))
    do_xin(0, (0,))
    col_ready(2)
    xin_ready(1)
    rest = tuple(range(1, T))
    for t in rest:
        rights[t].wait_recv()
    do_col(0, rest)
    do_col(1, rest)
    do_xin(0, rest)
    every = tuple(range(T))
    do_col(2, every)
    for k in range(3, Z):
        col_ready(k)
        xin_ready(k - 1)
        do_xin(k - 2, every)
        do_col(k, every)
    do_xin(Z - 2, every)
    xin_ready(Z - 1)
    do_xin(Z - 1, every)

    pairs = Z * X
    cross, xc, zc = {}, {}, {}

    def stage_a(q):
        t, j0 = q // JH, (q % JH) * JW

        def one(j, carry):
            at = pl.ds(pl.multiple_of(j0 + j * 256, 256), 256)
            carried = dot(kern[t], rows[:, at], 1, 0).astype(BF16)
            to = pl.ds(pl.multiple_of(j * 256, 256), 256)
            sig[q, :, to] = dot(own[...], carried, 0, 0)
            return carry
        lax.fori_loop(0, JW // 256, one, 0)
        for g in range(pairs):
            at = pl.ds(pl.multiple_of((g * 2 + 1 - c) * OUT, OUT), OUT)
            csend[q, g] = sig[q, at, :].astype(BF16)
        cross[q] = send(csend.at[q], crecv.at[q], rc_s.at[q], rc_r.at[q], aux=sibling)

    def summed(q, g):
        at = pl.ds(pl.multiple_of((g * 2 + c) * OUT, OUT), OUT)
        return sig[q, at, :] + crecv[q, g].astype(F32)

    def stage_b(q):
        cross[q].wait_recv()
        for e in range(1, X):
            for zz in range(Z):
                xsend[q, e - 1, zz] = summed(q, zz * X + xo(e)).astype(BF16)
            xc[q, e] = send(xsend.at[q, e - 1], xrecv.at[q, e - 1], rx_s.at[q, e - 1],
                            rx_r.at[q, e - 1], aux=dev(z, xo(e), c))

    def stage_c(q):
        for e in range(1, X):
            xc[q, e].wait_recv()
        for f in list(range(1, Z)) + [0]:
            value = summed(q, zo(f) * X + x)
            for e in range(1, X):
                value = value + xrecv[q, e - 1, zo(f)].astype(F32)
            if f == 0:
                fin[q] = value
            else:
                zsend[q, f - 1] = value.astype(BF16)
                zc[q, f] = send(zsend.at[q, f - 1], zrecv.at[q, f - 1], rz_s.at[q, f - 1],
                                rz_r.at[q, f - 1], aux=dev(zo(f), x, c))

    def stage_d(q):
        value = fin[q]
        for f in range(1, Z):
            zc[q, f].wait_recv()
            value = value + zrecv[q, f - 1].astype(F32)
        out[q // JH, :, pl.ds((q % JH) * JW, JW)] = value

    Q = T * JH
    stage_a(0)
    for q in range(1, Q):
        stage_a(q)
        stage_b(q - 1)
    stage_b(Q - 1)
    stage_c(0)
    for q in range(1, Q):
        stage_c(q)
        stage_d(q - 1)
    stage_d(Q - 1)
    for copy in sent:
        copy.wait_send()


def local(green, factors, pattern, coulomb):
    n = lax.axis_size("aux")
    T, O, _ = green.shape
    R = factors.shape[0]
    A = n * R
    chips = n // 2
    Z = 4
    X = chips // Z
    JH = 2
    JW = O // JH
    Q = T * JH
    OUT = O // n
    dma = pltpu.SemaphoreType.DMA
    vm = pltpu.VMEM
    scratch = [
        vm((R, O), BF16), vm((A, O), BF16), vm((n, 1, R), F32), vm((T, O, O), BF16),
        vm((T, 2 * R, O), BF16), vm((T, R, O), BF16), vm((R, R), F32), vm((T, R, A), BF16),
        vm((Q, O, JW), F32), vm((Q, chips, OUT, JW), BF16), vm((Q, chips, OUT, JW), BF16),
        vm((Q, X - 1, Z, OUT, JW), BF16), vm((Q, X - 1, Z, OUT, JW), BF16),
        vm((Q, Z - 1, OUT, JW), BF16), vm((Q, Z - 1, OUT, JW), BF16), vm((Q, OUT, JW), F32),
        dma((T,)),
        dma((Z - 1, 2)), dma((Z - 1, 2)),
        dma((Z, X - 1, 2)), dma((Z, X - 1, 2)),
        dma((Z, 2)), dma((Z, 2)),
        dma((Z, X - 1, 2)), dma((Z, X - 1, 2)),
        dma((T,)), dma((T,)),
        dma((Q,)), dma((Q,)),
        dma((Q, X - 1)), dma((Q, X - 1)),
        dma((Q, Z - 1)), dma((Q, Z - 1)),
    ]
    vmem = pl.BlockSpec(memory_space=pltpu.VMEM)
    result = pl.pallas_call(
        functools.partial(kernel, (Z, X, JH)),
        out_shape=jax.ShapeDtypeStruct((T, OUT, O), F32),
        in_specs=[pl.BlockSpec(memory_space=pltpu.SMEM), vmem, vmem,
                  pl.BlockSpec(memory_space=pl.ANY)],
        out_specs=vmem,
        scratch_shapes=scratch,
        compiler_params=pltpu.CompilerParams(
            collective_id=0, has_side_effects=True, vmem_limit_bytes=60 * 2**20),
    )(pattern, factors, coulomb.reshape(1, R), green)
    return jnp.transpose(result, (1, 0, 2))


def solution(mesh):
    in_specs = (P("tm", None, None), P("aux", None), P("aux", None), P("aux"))
    out_specs = P("aux", "tm", None)
    return jax.shard_map(local, mesh=mesh, in_specs=in_specs, out_specs=out_specs, check_vma=False)
```

time: 233 us -> 98.4 us (0.42)
  waiting for transfers between devices: 149 us -> 0 us
  Pallas kernels: 0 us -> 96 us
  matrix products: 38.3 us -> 0 us
  blocking collectives: 22.4 us -> 0 us
  between operations: 13.4 us -> 0.01 us
  starting transfers between devices: 3.1 us -> 0 us
  other arithmetic: 2.62 us -> 0 us
    reduce_scatter x1 -> x0, waiting for transfers between devices: 102 us -> none  [local(): lax.psum_scatter(-jnp.einsum('pi,tpj->itj', masked, carried, preferred_el...]
    pallas_call x0 -> x1, Pallas kernels: none -> 96 us  [local(): pl.pallas_call(functools.partial(kernel, (Z, X, JH)), out_shape=jax.Shape...]
    all_gather x1 -> x0, waiting for transfers between devices: 46.9 us -> none  [local(): rows = lax.all_gather(masked, 'aux', axis=0, tiled=True)]
    dot_general x5 -> x0, matrix products: 38.3 us -> none  [the longest x1 12.4 us: local(): jnp.einsum('tpo,qo->tpq', left, rows, preferred_element_type=jnp.float32)]
    all_gather x1 -> x0, blocking collectives: 22.4 us -> none  [local(): lax.all_gather(coulomb.astype(jnp.bfloat16), 'aux', axis=0, tiled=True)]
    ppermute x1 -> x0, starting transfers between devices: 3.06 us -> none  [swapped(): lax.ppermute(value, axis, [(i, i ^ 1 << distance) for i in range(lax.axis...]
  transfers between devices with their start and end apart: 3 -> 0, of which waited for: 2 -> 0; matrix products, arithmetic and copies ran while one was open for 7% -> 0% of each run, Pallas kernels for 0% -> 0%
where the time goes in v1:
time: 98.4 us; the launch traced here: 98.2 us
  Pallas kernels  96 us (98%)
  local copies, waits for them, and re-layouts  2.24 us (2%)
    pallas_call x1, Pallas kernels, local(): pl.pallas_call(functools.partial(kernel, (Z, X, JH)), out_shape=jax.Shape...  96 us
    transpose x1, local copies, waits for them, and re-layouts, local(): return jnp.transpose(result, (1, 0, 2))  2.24 us

profile of v1, /device:TPU:0, one launch (start us, length us, event | category | flops | bytes accessed | tf_op | source)
XLA Modules:
  0.0 98.2 jit_solution(12678066517859426946)
XLA Ops:
  0.0 96.0 %shard_map.46 = f32[2,64,1024]{2,1,0:T(8,128)} custom-call(s32[2,8]{1,0:T(2,128)} %pattern.1, bf16[256,1024]{1,0:T(8,128)(2,1)} %factors.1, f32[1,256]{1,0:T(1,128)} %bitcast.3, bf16[2,1024,1024]{2,1,0:T(8,128)(2,1)} %green_hbm.1), custom_call_target="tpu_custom_call" | custom-call | tf_op jit(solution)/shard_map/pallas_call | solution.py:292
  96.0 2.2 %copy.5 = f32[64,2,1024]{2,1,0:T(2,128)} copy(f32[64,2,1024]{2,0,1:T(8,128)} %bitcast.2) | data formatting | bytes 1048576 | tf_op jit(solution)/shard_map/transpose | solution.py:302

commit v2 on v1

--- a/solution.py
+++ b/solution.py
@@ -21,9 +21,10 @@
 
 def kernel(cfg, pattern, factors, coul, green_hbm, out, own, rows, weights, green, left_right,
            own_right, cp, kern, sig, csend, crecv, xsend, xrecv, zsend, zrecv, fin,
-           gsem, ring_s, ring_r, x_s, x_r, cc_s, cc_r, cx_s, cx_r, tm_s, tm_r,
+           gsem, ring_s, ring_r, x_s, x_r, y_s, y_r, cc_s, cc_r, cx_s, cx_r,
+           wring_s, wring_r, wx_s, wx_r, wcc_s, wcc_r, wcx_s, wcx_r, tm_s, tm_r,
            rc_s, rc_r, rx_s, rx_r, rz_s, rz_r):
-    Z, X, JH = cfg
+    Z, X, JH, H = cfg
     T, O = green.shape[0], green.shape[1]
     R = own.shape[0]
     JW = O // JH
@@ -45,6 +46,8 @@
         return lax.rem(z + f, Z)
 
     partner = lax.rem(tmi + tms // 2, tms)
+    plane = lax.rem(tmi, 2)
+    mate = tmi + 1 - 2 * plane
     sibling = dev(z, x, 1 - c)
     sent = []
 
@@ -75,11 +78,15 @@
     friends = [{"aux": dev(zo(f), x, c)} for f in range(1, Z)]
     friends += [{"aux": dev(z, xo(e), c)} for e in range(1, X)]
     friends += [{"aux": sibling}, {"tm": partner}]
+    if tms > 2 and tms % 2 == 0:
+        friends += [{"tm": mate}]
     for where in friends:
         pl.semaphore_signal(barrier, inc=1, device_id=where, device_id_type=MESH)
     pl.semaphore_wait(barrier, len(friends))
 
     nextd = dev(turned(lax.rem(pos + 1, Z)), x, c)
+    PR = R // H
+    shared = ()
 
     def col_owner(k):
         return dev(turned(lax.rem(pos + Z - k, Z)), x, c)
@@ -87,33 +94,68 @@
     def xin_owner(k, e):
         return dev(turned(lax.rem(pos + Z - k, Z)), lax.rem(x + X - e, X), c)
 
-    def pass_on(owner, s, r, to, first=False):
-        at = pl.ds(pl.multiple_of(owner * R, R), R)
-        src_rows = own if first else rows.at[at]
-        src_w = coul if first else weights.at[owner]
-        return [send(src_rows, rows.at[at], s.at[0], r.at[0], aux=to),
-                send(src_w, weights.at[owner], s.at[1], r.at[1], aux=to)]
-
-    ring, xs, ccs, cxs = {}, {}, {}, {}
+    def pass_piece(owner, h, s, r, first=False, **where):
+        at = pl.ds(pl.multiple_of(owner * R + h * PR, PR), PR)
+        src = own.at[pl.ds(pl.multiple_of(h * PR, PR), PR)] if first else rows.at[at]
+        return send(src, rows.at[at], s, r, **where)
+
+    def pass_weight(owner, s, r, first=False, **where):
+        return send(coul if first else weights.at[owner], weights.at[owner], s, r, **where)
+
+    ring, xs, ys, ccs, cxs = {}, {}, {}, {}, {}
+    wring, wxs, wccs, wcxs = {}, {}, {}, {}
 
     def wait_all(copies):
         for copy in copies:
             copy.wait_recv()
 
-    def col_ready(k):
+    def col(k, h):
         if k > 0:
-            wait_all(ring[k])
-        owner = col_owner(k)
+            ring[k, h].wait_recv()
+            if h == 0:
+                wring[k].wait_recv()
+        owner, first = col_owner(k), k == 0
         if k < Z - 1:
-            ring[k + 1] = pass_on(owner, ring_s.at[k], ring_r.at[k], nextd, k == 0)
-        for e in range(1, X):
-            xs[k, e] = pass_on(owner, x_s.at[k, e - 1], x_r.at[k, e - 1], dev(z, xo(e), c), k == 0)
-        ccs[k] = pass_on(owner, cc_s.at[k], cc_r.at[k], sibling, k == 0)
-
-    def xin_ready(k):
-        for e in range(1, X):
-            wait_all(xs[k, e])
-            cxs[k, e] = pass_on(xin_owner(k, e), cx_s.at[k, e - 1], cx_r.at[k, e - 1], sibling)
+            ring[k + 1, h] = pass_piece(owner, h, ring_s.at[k, h], ring_r.at[k, h], first, aux=nextd)
+        for e in range(1, X):
+            to = dev(z, xo(e), c)
+            if k not in shared:
+                xs[k, e, h] = pass_piece(owner, h, x_s.at[k, e - 1, h], x_r.at[k, e - 1, h], first,
+                                         aux=to)
+            elif h % 2:
+                i = h // 2
+                xs[k, e, i] = pass_piece(owner, 2 * i + plane, x_s.at[k, e - 1, i],
+                                         x_r.at[k, e - 1, i], first, aux=to)
+        ccs.setdefault(k, []).append(
+            pass_piece(owner, h, cc_s.at[k, h], cc_r.at[k, h], first, aux=sibling))
+        if h == 0:
+            if k < Z - 1:
+                wring[k + 1] = pass_weight(owner, wring_s.at[k], wring_r.at[k], first, aux=nextd)
+            for e in range(1, X):
+                wxs[k, e] = pass_weight(owner, wx_s.at[k, e - 1], wx_r.at[k, e - 1], first,
+                                        aux=dev(z, xo(e), c))
+            ccs[k].append(pass_weight(owner, wcc_s.at[k], wcc_r.at[k], first, aux=sibling))
+
+    def xin(k, i):
+        for e in range(1, X):
+            owner = xin_owner(k, e)
+            xs[k, e, i].wait_recv()
+            h, n = i, i
+            if k in shared:
+                h, n = 2 * i + plane, 2 * i
+                ys[k, e, i] = pass_piece(owner, h, y_s.at[k, e - 1, i], y_r.at[k, e - 1, i], tm=mate)
+            mine = cxs.setdefault((k, e), [])
+            mine.append(pass_piece(owner, h, cx_s.at[k, e - 1, n], cx_r.at[k, e - 1, n], aux=sibling))
+            if i == 0:
+                wxs[k, e].wait_recv()
+                mine.append(pass_weight(owner, wcx_s.at[k, e - 1], wcx_r.at[k, e - 1], aux=sibling))
+
+    def yin(k, i):
+        for e in range(1, X):
+            ys[k, e, i].wait_recv()
+            cxs[k, e].append(
+                pass_piece(xin_owner(k, e), 2 * i + 1 - plane, cx_s.at[k, e - 1, 2 * i + 1],
+                           cx_r.at[k, e - 1, 2 * i + 1], aux=sibling))
 
     waited = set()
 
@@ -162,35 +204,55 @@
             return carry
         lax.fori_loop(0, O // 256, one, 0)
 
-    col_ready(0)
+    for h in range(H):
+        col(0, h)
     for t in range(T):
         project_right(t)
     for t in range(T):
         project_left(t)
-    col_ready(1)
-    xin_ready(0)
-    rights[0].wait_recv()
-    do_col(0, (0,))
-    do_col(1, (0,))
-    do_xin(0, (0,))
-    col_ready(2)
-    xin_ready(1)
-    rest = tuple(range(1, T))
-    for t in rest:
-        rights[t].wait_recv()
-    do_col(0, rest)
-    do_col(1, rest)
-    do_xin(0, rest)
-    every = tuple(range(T))
-    do_col(2, every)
-    for k in range(3, Z):
-        col_ready(k)
-        xin_ready(k - 1)
-        do_xin(k - 2, every)
-        do_col(k, every)
-    do_xin(Z - 2, every)
-    xin_ready(Z - 1)
-    do_xin(Z - 1, every)
+
+    rest, every = tuple(range(1, T)), tuple(range(T))
+    todo = []
+
+    def plan(when, what, *args):
+        todo.append((when, len(todo), what, args))
+
+    lag = 0.7
+    for k in range(1, Z):
+        for h in range(H):
+            plan((k - 1) * H + h + 1 + lag * k, col, k, h)
+    last = 0.0
+    for k in range(Z):
+        if k in shared:
+            for i in range(H // 2):
+                ready = (k - 1) * H + 2 * i + 2 + lag * k
+                last = max(last + 1, ready + 1 + lag)
+                plan(last, xin, k, i)
+                plan(max(last + 1 + lag, 11.7 + i), yin, k, i)
+        else:
+            for i in range(H):
+                last = k * H + i + 1 + lag
+                plan(last, xin, k, i)
+    plan(6.5, lambda: rights[0].wait_recv())
+    plan(6.6, do_col, 0, (0,))
+    plan(6.7, do_col, 1, (0,))
+    plan(6.8, do_xin, 0, (0,))
+    plan(9.3, do_xin, 1, (0,))
+    plan(9.6, do_col, 2, (0,))
+    plan(10.6, lambda: [rights[t].wait_recv() for t in rest])
+    plan(10.61, do_col, 0, rest)
+    plan(10.8, do_col, 1, rest)
+    plan(11.2, do_xin, 0, rest)
+    plan(11.9, do_xin, 1, rest)
+    plan(12.3, do_col, 2, rest)
+    tail = 13.3
+    for k in range(2, Z):
+        if k > 2:
+            plan(max(tail, (k - 1) * H + H + lag * k + 0.5), do_col, k, every)
+        full = max([w for w, _, f, g in todo if f in (xin, yin) and g[0] == k])
+        plan(full + 0.4, do_xin, k, every)
+    for _, _, what, args in sorted(todo, key=lambda item: item[:2]):
+        what(*args)
 
     pairs = Z * X
     cross, xc, zc = {}, {}, {}
@@ -244,16 +306,16 @@
         out[q // JH, :, pl.ds((q % JH) * JW, JW)] = value
 
     Q = T * JH
-    stage_a(0)
-    for q in range(1, Q):
-        stage_a(q)
-        stage_b(q - 1)
-    stage_b(Q - 1)
-    stage_c(0)
-    for q in range(1, Q):
-        stage_c(q)
-        stage_d(q - 1)
-    stage_d(Q - 1)
+    todo.clear()
+    step, hop = 10.4 / Q, 22.5 / Q
+    for q in range(Q):
+        plan(step * (q + 1), stage_a, q)
+        plan(step * (q + 2) + 0.1, stage_b, q)
+        arrived = 2 * step + 1 + hop * (q + 1) + 1.5
+        plan(arrived, stage_c, q)
+        plan(arrived + hop + 2.5, stage_d, q)
+    for _, _, what, args in sorted(todo, key=lambda item: item[:2]):
+        what(*args)
     for copy in sent:
         copy.wait_send()
 
@@ -267,6 +329,7 @@
     Z = 4
     X = chips // Z
     JH = 2
+    H = 4
     JW = O // JH
     Q = T * JH
     OUT = O // n
@@ -279,10 +342,13 @@
         vm((Q, X - 1, Z, OUT, JW), BF16), vm((Q, X - 1, Z, OUT, JW), BF16),
         vm((Q, Z - 1, OUT, JW), BF16), vm((Q, Z - 1, OUT, JW), BF16), vm((Q, OUT, JW), F32),
         dma((T,)),
-        dma((Z - 1, 2)), dma((Z - 1, 2)),
-        dma((Z, X - 1, 2)), dma((Z, X - 1, 2)),
-        dma((Z, 2)), dma((Z, 2)),
-        dma((Z, X - 1, 2)), dma((Z, X - 1, 2)),
+        dma((Z - 1, H)), dma((Z - 1, H)),
+        dma((Z, X - 1, H)), dma((Z, X - 1, H)),
+        dma((Z, X - 1, H // 2)), dma((Z, X - 1, H // 2)),
+        dma((Z, H)), dma((Z, H)),
+        dma((Z, X - 1, H)), dma((Z, X - 1, H)),
+        dma((Z - 1,)), dma((Z - 1,)), dma((Z, X - 1)), dma((Z, X - 1)),
+        dma((Z,)), dma((Z,)), dma((Z, X - 1)), dma((Z, X - 1)),
         dma((T,)), dma((T,)),
         dma((Q,)), dma((Q,)),
         dma((Q, X - 1)), dma((Q, X - 1)),
@@ -290,7 +356,7 @@
     ]
     vmem = pl.BlockSpec(memory_space=pltpu.VMEM)
     result = pl.pallas_call(
-        functools.partial(kernel, (Z, X, JH)),
+        functools.partial(kernel, (Z, X, JH, H)),
         out_shape=jax.ShapeDtypeStruct((T, OUT, O), F32),
         in_specs=[pl.BlockSpec(memory_space=pltpu.SMEM), vmem, vmem,
                   pl.BlockSpec(memory_space=pl.ANY)],

time: 98.4 us -> 96.9 us (0.985)
  Pallas kernels: 96 us -> 94.4 us
    pallas_call x1, Pallas kernels: 96 us -> 94.4 us  [local(): pl.pallas_call(functools.partial(kernel, (Z, X, JH, H)), out_shape=jax.Sh...]
where the time goes in v2:
time: 96.9 us; the launch traced here: 96.7 us
  Pallas kernels  94.4 us (97%)
  local copies, waits for them, and re-layouts  2.24 us (2%)
    pallas_call x1, Pallas kernels, local(): pl.pallas_call(functools.partial(kernel, (Z, X, JH, H)), out_shape=jax.Sh...  94.4 us
    transpose x1, local copies, waits for them, and re-layouts, local(): return jnp.transpose(result, (1, 0, 2))  2.24 us

profile of v2, /device:TPU:0, one launch (start us, length us, event | category | flops | bytes accessed | tf_op | source)
XLA Modules:
  0.0 96.7 jit_solution(2775599435039426544)
XLA Ops:
  0.0 94.4 %shard_map.46 = f32[2,64,1024]{2,1,0:T(8,128)} custom-call(s32[2,8]{1,0:T(2,128)} %pattern.1, bf16[256,1024]{1,0:T(8,128)(2,1)} %factors.1, f32[1,256]{1,0:T(1,128)} %bitcast.3, bf16[2,1024,1024]{2,1,0:T(8,128)(2,1)} %green_hbm.1), custom_call_target="tpu_custom_call" | custom-call | tf_op jit(solution)/shard_map/pallas_call | solution.py:358
  94.5 2.2 %copy.5 = f32[64,2,1024]{2,1,0:T(2,128)} copy(f32[64,2,1024]{2,0,1:T(8,128)} %bitcast.2) | data formatting | bytes 1048576 | tf_op jit(solution)/shard_map/transpose | solution.py:368

commit v3 on v2

--- a/solution.py
+++ b/solution.py
@@ -86,7 +86,7 @@
 
     nextd = dev(turned(lax.rem(pos + 1, Z)), x, c)
     PR = R // H
-    shared = ()
+    shared = (1,) if tms % 2 == 0 else ()
 
     def col_owner(k):
         return dev(turned(lax.rem(pos + Z - k, Z)), x, c)
@@ -237,13 +237,13 @@
     plan(6.6, do_col, 0, (0,))
     plan(6.7, do_col, 1, (0,))
     plan(6.8, do_xin, 0, (0,))
-    plan(9.3, do_xin, 1, (0,))
+    plan(13.3, do_xin, 1, (0,))
     plan(9.6, do_col, 2, (0,))
     plan(10.6, lambda: [rights[t].wait_recv() for t in rest])
     plan(10.61, do_col, 0, rest)
     plan(10.8, do_col, 1, rest)
     plan(11.2, do_xin, 0, rest)
-    plan(11.9, do_xin, 1, rest)
+    plan(13.35, do_xin, 1, rest)
     plan(12.3, do_col, 2, rest)
     tail = 13.3
     for k in range(2, Z):

time: 96.9 us -> 93.1 us (0.961)
  Pallas kernels: 94.4 us -> 90.7 us
    pallas_call x1, Pallas kernels: 94.4 us -> 90.7 us  [local(): pl.pallas_call(functools.partial(kernel, (Z, X, JH, H)), out_shape=jax.Sh...]
where the time goes in v3:
time: 93.1 us; the launch traced here: 92.9 us
  Pallas kernels  90.7 us (97%)
  local copies, waits for them, and re-layouts  2.24 us (2%)
    pallas_call x1, Pallas kernels, local(): pl.pallas_call(functools.partial(kernel, (Z, X, JH, H)), out_shape=jax.Sh...  90.7 us
    transpose x1, local copies, waits for them, and re-layouts, local(): return jnp.transpose(result, (1, 0, 2))  2.24 us

profile of v3, /device:TPU:0, one launch (start us, length us, event | category | flops | bytes accessed | tf_op | source)
XLA Modules:
  0.0 92.9 jit_solution(2563329152193536788)
XLA Ops:
  0.0 90.7 %shard_map.46 = f32[2,64,1024]{2,1,0:T(8,128)} custom-call(s32[2,8]{1,0:T(2,128)} %pattern.1, bf16[256,1024]{1,0:T(8,128)(2,1)} %factors.1, f32[1,256]{1,0:T(1,128)} %bitcast.3, bf16[2,1024,1024]{2,1,0:T(8,128)(2,1)} %green_hbm.1), custom_call_target="tpu_custom_call" | custom-call | tf_op jit(solution)/shard_map/pallas_call | solution.py:358
  90.7 2.2 %copy.5 = f32[64,2,1024]{2,1,0:T(2,128)} copy(f32[64,2,1024]{2,0,1:T(8,128)} %bitcast.2) | data formatting | bytes 1048576 | tf_op jit(solution)/shard_map/transpose | solution.py:368

commit v4 on v3

--- a/solution.py
+++ b/solution.py
@@ -28,7 +28,7 @@
     T, O = green.shape[0], green.shape[1]
     R = own.shape[0]
     JW = O // JH
-    OUT = out.shape[1]
+    OUT = out.shape[0]
     tms = lax.axis_size("tm")
     a, tmi = lax.axis_index("aux"), lax.axis_index("tm")
     c = lax.rem(a, 2)
@@ -303,7 +303,7 @@
         for f in range(1, Z):
             zc[q, f].wait_recv()
             value = value + zrecv[q, f - 1].astype(F32)
-        out[q // JH, :, pl.ds((q % JH) * JW, JW)] = value
+        out[:, q // JH, pl.ds((q % JH) * JW, JW)] = value
 
     Q = T * JH
     todo.clear()
@@ -357,7 +357,7 @@
     vmem = pl.BlockSpec(memory_space=pltpu.VMEM)
     result = pl.pallas_call(
         functools.partial(kernel, (Z, X, JH, H)),
-        out_shape=jax.ShapeDtypeStruct((T, OUT, O), F32),
+        out_shape=jax.ShapeDtypeStruct((OUT, T, O), F32),
         in_specs=[pl.BlockSpec(memory_space=pltpu.SMEM), vmem, vmem,
                   pl.BlockSpec(memory_space=pl.ANY)],
         out_specs=vmem,
@@ -365,7 +365,7 @@
         compiler_params=pltpu.CompilerParams(
             collective_id=0, has_side_effects=True, vmem_limit_bytes=60 * 2**20),
     )(pattern, factors, coulomb.reshape(1, R), green)
-    return jnp.transpose(result, (1, 0, 2))
+    return result
 
 
 def solution(mesh):

time: 93.1 us -> 92.7 us (level)
    transpose x1 -> x0, local copies, waits for them, and re-layouts: 2.24 us -> none  [local(): return jnp.transpose(result, (1, 0, 2))]
    unnamed x0 -> x1, local copies, waits for them, and re-layouts: none -> 1.87 us
where the time goes in v4:
time: 92.7 us; the launch traced here: 92.6 us
  Pallas kernels  90.7 us (98%)
  local copies, waits for them, and re-layouts  1.87 us (2%)
    pallas_call x1, Pallas kernels, local(): pl.pallas_call(functools.partial(kernel, (Z, X, JH, H)), out_shape=jax.Sh...  90.7 us
    unnamed x1, local copies, waits for them, and re-layouts  1.87 us

profile of v4, /device:TPU:0, one launch (start us, length us, event | category | flops | bytes accessed | tf_op | source)
XLA Modules:
  0.0 92.6 jit_solution(17698554664118775520)
XLA Ops:
  0.0 90.7 %shard_map.46 = f32[64,2,1024]{2,1,0:T(2,128)} custom-call(s32[2,8]{1,0:T(2,128)} %pattern.1, bf16[256,1024]{1,0:T(8,128)(2,1)} %factors.1, f32[1,256]{1,0:T(1,128)} %bitcast.1, bf16[2,1024,1024]{2,1,0:T(8,128)(2,1)} %green_hbm.1), custom_call_target="tpu_custom_call" | custom-call | tf_op jit(solution)/shard_map/pallas_call | solution.py:358
  90.7 1.9 %copy.6 = f32[64,2,1024]{2,1,0:T(2,128)} copy(f32[64,2,1024]{2,1,0:T(2,128)} %shard_map.46) | data formatting | bytes 1048576
